TPU v7x, 32 devices: a whole 2x2x4 slice. The times are simulated.
32 devices in a mesh: lb: 8 (over y, x, core), rb: 4 (over z).
Axes of the slice: x: 2, y: 2, z: 4, core: 2. Of those that a mesh axis runs over, the one named last changes fastest.
Arguments:
- wavefunction: bfloat16 [3072, 4, 3072], P('lb', None, 'rb'), may hold values from -6 to 6
- left_environment: bfloat16 [8, 1024, 3072], P(None, 'lb'), may hold values from -0.109375 to 0.109375
- operator_left: float32 [8, 8, 2, 2], replicated, may hold values from -1.5 to 1.5
- operator_right: float32 [8, 8, 2, 2], replicated, may hold values from -1.5 to 1.5
- right_environment: bfloat16 [8, 3072, 3072], P(None, 'rb', 'lb'), may hold values from -0.0546875 to 0.0546875
- row_sector: int32 [8], replicated, may hold values from 0 to 3, never falling along the last dimension, each value on 1 to 4 neighbouring positions
Outputs:
- applied_state: bfloat16 [1024, 4, 3072], P('lb', None, 'rb')
- density: float32 [1024, 1024], P('lb', 'rb')
Inputs may be any that keep to these rules, and one draw needn't show every extreme that they name: `row_sector`: entry t is the sector of output rows t * 128 to (t + 1) * 128 - 1. Entries never fall along t; each sector holds 1 to 4 tiles, and one holds exactly 4.
All inputs are finite; a program needn't handle non-finite values.
Results may differ from a plain program's by a relative error of at most 0.013.
Values may be sent and summed in bfloat16 or wider, within the bound.
No kernel may reach another device: no remote copies, remote signals or barrier semaphores. Data moves between devices by JAX's collectives and lax.ppermute only.
A program may use at most 128 MiB of HBM per device.

v0:
```python
import math
import jax
import jax.numpy as jnp
from jax import lax
from jax.sharding import PartitionSpec as P

BOND_WIDTH = 3072
SECTOR_TILES = 4


def shifted(value, axis, by):
    devices = lax.axis_size(axis)
    pairs = [(i, i + by) for i in range(devices) if 0 <= i + by < devices]
    return lax.ppermute(value, axis, pairs)


def combine_operators(operator_left, operator_right):
    channels = operator_left.shape[0]
    joined = jnp.einsum(
        "aups,uvqt->avpqst", operator_left, operator_right, precision=lax.Precision.HIGHEST
    )
    return joined.reshape(channels, channels, 4, 4)


def label_at(labels, position):
    matches = jnp.arange(labels.shape[0], dtype=jnp.int32) == position
    return (jnp.sum(jnp.where(matches, labels, 0)), jnp.any(matches))


def tile_gram(left_tile, right_tile):
    return lax.dot_general(
        left_tile, right_tile, (((1,), (1,)), ((), ())), preferred_element_type=jnp.float32
    )


def fetch_tile(own_tile, offset):
    return shifted(own_tile, "lb", -offset)


def shards(
    wavefunction, left_environment, operator_left, operator_right, right_environment, row_sector
):
    channels, row_count, full_bond = left_environment.shape
    local_right = wavefunction.shape[2]
    left_matrix = left_environment.reshape(channels * row_count, full_bond)
    rows_piece = lax.all_gather(wavefunction, "lb", axis=0, tiled=True)
    flat_piece = rows_piece.reshape(rows_piece.shape[0], 4 * local_right)
    left_part = jnp.dot(left_matrix, flat_piece, preferred_element_type=jnp.float32)
    left_part = left_part.reshape(channels, row_count, 4, local_right)
    combined = combine_operators(operator_left, operator_right)
    mixed_part = jnp.einsum(
        "avyx,alxr->lyvr", combined, left_part, precision=lax.Precision.HIGHEST
    ).astype(jnp.bfloat16)
    mixed_matrix = mixed_part.reshape(row_count * 4, channels * local_right)
    columns_piece = lax.all_gather(right_environment, "lb", axis=2, tiled=True)
    flat_piece = columns_piece.reshape(channels * local_right, columns_piece.shape[2])
    partial_value = jnp.dot(mixed_matrix, flat_piece, preferred_element_type=jnp.float32)
    summed = lax.psum_scatter(
        partial_value.astype(jnp.bfloat16), "rb", scatter_dimension=1, tiled=True
    ).astype(jnp.float32)
    applied = summed.astype(jnp.bfloat16).reshape(row_count, 4, summed.shape[1])
    own_tile = applied.reshape(row_count, 4 * summed.shape[1])
    own_index = lax.axis_index("lb")
    tile_count = lax.axis_size("lb")
    reach_tiles = SECTOR_TILES - 1
    own_label = label_at(row_sector, own_index)[0]
    buffer = jnp.zeros((row_count, (tile_count + 2 * reach_tiles) * row_count), jnp.float32)

    def place_block(buffer, gram_block, offset):
        mate_index = own_index + offset
        mate_label, inside = label_at(row_sector, mate_index)
        keep_block = jnp.logical_and(inside, mate_label == own_label)
        gram_block = jnp.where(keep_block, gram_block, jnp.float32(0.0))
        column_start = (mate_index + reach_tiles) * row_count
        return lax.dynamic_update_slice(buffer, gram_block, (jnp.int32(0), column_start))

    buffer = place_block(buffer, tile_gram(own_tile, own_tile), 0)
    for distance in range(1, SECTOR_TILES):
        gram_block = tile_gram(own_tile, fetch_tile(own_tile, distance))
        buffer = place_block(buffer, gram_block, distance)
        returned = shifted(gram_block.astype(jnp.bfloat16), "lb", distance).astype(gram_block.dtype)
        buffer = place_block(buffer, returned.T, -distance)
    full_rows = buffer[:, reach_tiles * row_count : (reach_tiles + tile_count) * row_count]
    density = lax.psum_scatter(
        full_rows.astype(jnp.bfloat16), "rb", scatter_dimension=1, tiled=True
    ).astype(jnp.float32) * (1.0 / math.sqrt(4.0 * BOND_WIDTH))
    return (applied, density)


def solution(mesh):
    placed = (P("lb", None, "rb"), P(None, "lb", None), P(), P(), P(None, "rb", "lb"), P())
    return jax.shard_map(
        shards,
        mesh=mesh,
        in_specs=placed,
        out_specs=(P("lb", None, "rb"), P("lb", "rb")),
        check_vma=False,
    )
```

profile of v0, /device:TPU:0, one launch (start us, length us, event | category | flops | bytes accessed | tf_op | source)
XLA Modules:
  0.0 471.0 jit_solution(350183610917870450)
XLA Ops:
  7.2 0.0 copy-start
  7.2 0.0 all-gather.3.cloned.1.call-start
  7.2 0.7 all-gather.3.cloned.1.call-update
  7.9 0.0 all-gather.5.cloned.1.call-start
  8.0 0.7 all-gather.5.cloned.1.call-update
  8.7 0.0 reduce-scatter.3.cloned.1.call-start
  8.7 0.4 convolution_bitcast_fusion
  9.2 0.7 copy.24
  9.9 101.4 %all-gather.3.cloned.1.call-done = bf16[3072,4,768]{2,1,0:T(4,128)(2,1)} async-done(((bf16[384,4,768]{2,1,0:T(4,128)(2,1)}), bf16[3072,4,768]{2,1,0:T(4,128)(2,1)}) %all-gather.3.cloned.1.call-update) | async-done | bytes 18874384 | tf_op jit(solution)/shard_map/all_gather | solution.py:46
  111.2 29.9 %copy.37 = bf16[3072,4,768]{0,2,1:T(8,128)(2,1)} copy(bf16[3072,4,768]{2,1,0:T(4,128)(2,1)} %all-gather.3.cloned.1.call-done) | data formatting | bytes 37748736 | tf_op jit(solution)/shard_map/reshape | solution.py:47
  141.2 27.1 %fusion = f32[8,128,4,768]{3,0,2,1:T(8,128)S(1)} fusion(bf16[3072,4,768]{0,2,1:T(8,128)(2,1)} %copy.37, bf16[8,128,3072,1]{2,1,0,3:T(8,128)(2,1)} %bitcast.55), kind=kOutput, calls=%fused_computation | convolution fusion | flops 19327352832 | bytes 37748736 | tf_op jit(solution)/shard_map/dot_general | solution.py:48
  168.3 11.4 %bitcast_convert_fusion = bf16[128,768,8,4]{1,2,3,0:T(8,128)(2,1)S(1)} fusion(f32[8,8,4,4,1]{1,0,3,2,4:T(8,128)S(1)} %bitcast.52, f32[8,128,4,768]{3,0,2,1:T(8,128)S(1)} %fusion), kind=kOutput, calls=%fused_computation.4 | convolution fusion | flops 1211105280 | bytes 18878464 | tf_op jit(solution)/shard_map/avyx,alxr->lyvr/dot_general | solution.py:51
  179.7 4.6 copy.43
  184.3 115.8 %all-gather.5.cloned.1.call-done = bf16[8,768,3072]{2,1,0:T(8,128)(2,1)} async-done(((bf16[8,768,384]{2,1,0:T(8,128)(2,1)}), bf16[8,768,3072]{2,1,0:T(8,128)(2,1)}) %all-gather.5.cloned.1.call-update) | async-done | bytes 37748752 | tf_op jit(solution)/shard_map/all_gather | solution.py:55
  300.1 27.4 %convolution_convert_fusion = bf16[512,3072]{1,0:T(8,128)(2,1)} fusion(bf16[512,6144]{1,0:T(8,128)(2,1)} %bitcast.51, bf16[6144,3072]{1,0:T(8,128)(2,1)} %bitcast.54), kind=kOutput, calls=%fused_computation.6 | convolution fusion | flops 19328925696 | bytes 47185920 | tf_op jit(solution)/shard_map/dot_general | solution.py:57
  327.6 0.0 reduce-scatter.3.cloned.1.call-update
  327.6 0.0 copy-start.1
  327.6 0.0 reduce-scatter.5.cloned.1.call-start
  327.7 60.5 %reduce-scatter.3.cloned.1.call-done = bf16[512,768]{1,0:T(8,128)(2,1)} async-done(((bf16[512,3072]{1,0:T(8,128)(2,1)}), bf16[512,768]{1,0:T(8,128)(2,1)}) %reduce-scatter.3.cloned.1.call-update) | async-done | bytes 786448 | tf_op jit(solution)/shard_map/reduce_scatter | solution.py:58
  388.2 1.6 reshape_reshape.3
  389.8 1.3 collective-permute-start
  391.1 0.6 compare_reduce_fusion.6
  391.8 0.6 compare_reduce_fusion.5
  392.4 0.8 fusion.16
  395.1 1.3 collective-permute-start.2
  396.4 1.0 fusion.7
  397.5 0.4 select_dynamic-update-slice_fusion.2
  397.9 9.8 %collective-permute-start.1 = (bf16[128,128]{1,0:T(8,128)(2,1)S(1)}, bf16[128,128]{1,0:T(8,128)(2,1)S(1)}, u32[]{:S(2)}, u32[]{:S(2)}) collective-permute-start(bf16[128,128]{1,0:T(8,128)(2,1)S(1)} %get-tuple-element.10), channel_id=1, source_target_pairs={{0,4},{4,8},{8,12},{12,16},{16,20},{20,24},{24,28},{1,5},{5,9},{9,... | collective-permute-start | bytes 98312 | tf_op jit(solution)/shard_map/ppermute | solution.py:14
  407.7 0.6 compare_reduce_fusion.4
  408.3 0.6 compare_reduce_fusion.3
  412.8 1.3 collective-permute-start.4
  414.1 0.1 copy.26
  414.2 8.3 %collective-permute-done.2 = bf16[128,3072]{1,0:T(8,128)(2,1)} collective-permute-done((bf16[128,3072]{1,0:T(8,128)(2,1)S(1)}, bf16[128,3072]{1,0:T(8,128)(2,1)}, u32[]{:S(2)}, u32[]{:S(2)}) %collective-permute-start.2) | collective-permute-done | bytes 786464 | tf_op jit(solution)/shard_map/ppermute | solution.py:14
  422.5 1.5 select_dynamic-update-slice_fusion.1
  424.1 3.4 collective-permute-start.3
  427.5 0.6 compare_reduce_fusion.2
  428.1 0.6 compare_reduce_fusion.1
  432.7 0.1 copy.27
  432.8 0.4 select_dynamic-update-slice_fusion
  433.2 7.3 %collective-permute-start.5 = (bf16[128,128]{1,0:T(8,128)(2,1)S(1)}, bf16[128,128]{1,0:T(8,128)(2,1)S(1)}, u32[]{:S(2)}, u32[]{:S(2)}) collective-permute-start(bf16[128,128]{1,0:T(8,128)(2,1)S(1)} %get-tuple-element.14), channel_id=1, source_target_pairs={{0,12},{4,16},{8,20},{12,24},{16,28},{1,13},{5,17},{9,21},{13,25},... | collective-permute-start | bytes 98312 | tf_op jit(solution)/shard_map/ppermute | solution.py:14
  440.5 0.6 compare_reduce_fusion
  443.1 0.0 collective-permute-done.5
  443.1 0.1 copy.28
  443.2 0.7 slice.7
  444.0 0.0 reduce-scatter.5.cloned.1.call-update
  444.0 1.1 reshape.28
  445.1 17.8 %reduce-scatter.5.cloned.1.call-done = bf16[128,256]{1,0:T(8,128)(2,1)} async-done(((bf16[128,1024]{1,0:T(8,128)(2,1)}), bf16[128,256]{1,0:T(8,128)(2,1)}) %reduce-scatter.5.cloned.1.call-update) | async-done | bytes 65552 | tf_op jit(solution)/shard_map/reduce_scatter | solution.py:84
  462.9 1.5 convert_multiply_fusion
  (21 shorter events, 0.2 us)
Async XLA Ops:
  7.2 1.6 copy-start
  7.2 1.6 copy-start.4
  7.2 104.0 %all-gather.3.cloned.1.call-start = ((), (), s32[]{:S(2)}) async-start(), calls=%async_computation.2 | async-start | bytes 21233664 | tf_op jit(solution)/shard_map/all_gather | solution.py:46
  7.9 292.2 %all-gather.5.cloned.1.call-start = ((), (), s32[]{:S(2)}) async-start(), calls=%async_computation.3 | async-start | bytes 42467328 | tf_op jit(solution)/shard_map/all_gather | solution.py:55
  8.7 379.5 %reduce-scatter.3.cloned.1.call-start = ((), (), s32[]{:S(2)}) async-start(), calls=%async_computation.4 | async-start | bytes 3932160 | tf_op jit(solution)/shard_map/reduce_scatter | solution.py:58
  141.2 27.1 %copy-start.3 = (f32[8,8,2,2,2,2]{1,0,5,4,3,2:T(8,128)S(1)}, f32[8,8,2,2,2,2]{1,0,5,4,3,2:T(8,128)}, u32[]{:S(2)}) copy-start(f32[8,8,2,2,2,2]{1,0,5,4,3,2:T(8,128)} %copy.24) | copy-start | bytes 12292
  300.1 92.3 %copy-start.5 = (s32[8]{0:T(128)S(1)}, s32[8]{0:T(128)}, u32[]{:S(2)}) copy-start(s32[8]{0:T(128)} %param.11) | copy-start | bytes 100
  327.6 136.8 %copy-start.1 = (f32[8,8,2,2]{1,3,2,0:T(2,128)S(1)}, f32[8,8,2,2]{1,3,2,0:T(2,128)}, u32[]{:S(2)}) copy-start(f32[8,8,2,2]{1,3,2,0:T(2,128)} %param.8) | copy-start | bytes 3076
  327.6 135.3 %reduce-scatter.5.cloned.1.call-start = ((), (), s32[]{:S(2)}) async-start(), calls=%async_computation.5 | async-start | bytes 327680 | tf_op jit(solution)/shard_map/reduce_scatter | solution.py:84
  388.2 55.9 %copy-start.2 = (bf16[512,768]{1,0:T(8,128)(2,1)S(1)}, bf16[512,768]{1,0:T(8,128)(2,1)}, u32[]{:S(2)}) copy-start(bf16[512,768]{1,0:T(8,128)(2,1)} %reduce-scatter.3.cloned.1.call-done) | copy-start | bytes 2359300
  389.8 7.7 %collective-permute-start = (bf16[128,3072]{1,0:T(8,128)(2,1)S(1)}, bf16[128,3072]{1,0:T(8,128)(2,1)S(1)}, u32[]{:S(2)}, u32[]{:S(2)}) collective-permute-start(bf16[128,3072]{1,0:T(8,128)(2,1)S(1)} %reshape_reshape.3), channel_id=1, source_target_pairs={{4,0},{8,4},{12,8},{16,12},{20,16},{24,20},{28,24},{5,1},{9,5},{13... | collective-permute-start | bytes 2359304 | tf_op jit(solution)/shard_map/ppermute | solution.py:14
  395.1 27.4 %collective-permute-start.2 = (bf16[128,3072]{1,0:T(8,128)(2,1)S(1)}, bf16[128,3072]{1,0:T(8,128)(2,1)}, u32[]{:S(2)}, u32[]{:S(2)}) collective-permute-start(bf16[128,3072]{1,0:T(8,128)(2,1)S(1)} %reshape_reshape.3), channel_id=1, source_target_pairs={{8,0},{12,4},{16,8},{20,12},{24,16},{28,20},{9,1},{13,5},{17,9},{2... | collective-permute-start | bytes 2359304 | tf_op jit(solution)/shard_map/ppermute | solution.py:14
  397.9 16.2 %collective-permute-start.1 = (bf16[128,128]{1,0:T(8,128)(2,1)S(1)}, bf16[128,128]{1,0:T(8,128)(2,1)S(1)}, u32[]{:S(2)}, u32[]{:S(2)}) collective-permute-start(bf16[128,128]{1,0:T(8,128)(2,1)S(1)} %get-tuple-element.10), channel_id=1, source_target_pairs={{0,4},{4,8},{8,12},{12,16},{16,20},{20,24},{24,28},{1,5},{5,9},{9,... | collective-permute-start | bytes 98312 | tf_op jit(solution)/shard_map/ppermute | solution.py:14
  412.8 20.0 %collective-permute-start.4 = (bf16[128,3072]{1,0:T(8,128)(2,1)S(1)}, bf16[128,3072]{1,0:T(8,128)(2,1)S(1)}, u32[]{:S(2)}, u32[]{:S(2)}) collective-permute-start(bf16[128,3072]{1,0:T(8,128)(2,1)S(1)} %reshape_reshape.3), channel_id=1, source_target_pairs={{12,0},{16,4},{20,8},{24,12},{28,16},{13,1},{17,5},{21,9},{25,13},... | collective-permute-start | bytes 2359304 | tf_op jit(solution)/shard_map/ppermute | solution.py:14
  424.1 8.6 %collective-permute-start.3 = (bf16[128,128]{1,0:T(8,128)(2,1)S(1)}, bf16[128,128]{1,0:T(8,128)(2,1)S(1)}, u32[]{:S(2)}, u32[]{:S(2)}) collective-permute-start(bf16[128,128]{1,0:T(8,128)(2,1)S(1)} %get-tuple-element.12), channel_id=1, source_target_pairs={{0,8},{4,12},{8,16},{12,20},{16,24},{20,28},{1,9},{5,13},{9,17},{1... | collective-permute-start | bytes 98312 | tf_op jit(solution)/shard_map/ppermute | solution.py:14
  433.2 9.9 %collective-permute-start.5 = (bf16[128,128]{1,0:T(8,128)(2,1)S(1)}, bf16[128,128]{1,0:T(8,128)(2,1)S(1)}, u32[]{:S(2)}, u32[]{:S(2)}) collective-permute-start(bf16[128,128]{1,0:T(8,128)(2,1)S(1)} %get-tuple-element.14), channel_id=1, source_target_pairs={{0,12},{4,16},{8,20},{12,24},{16,28},{1,13},{5,17},{9,21},{13,25},... | collective-permute-start | bytes 98312 | tf_op jit(solution)/shard_map/ppermute | solution.py:14
Sparse Core Ops, SparseCore 0:
  9.9 101.3 all-gather.2
  113.1 186.9 all-gather.4
  327.7 60.3 reduce-scatter.2
  444.1 18.7 reduce-scatter.4
where the time goes:
time: 472 us; the launch traced here: 471 us
  waiting for transfers between devices  305 us (65%)
  matrix products  69.7 us (15%)
  local copies, waits for them, and re-layouts  39.2 us (8%)
  between operations  25.5 us (5%)
  starting transfers between devices  24.6 us (5%)
  other arithmetic  6.78 us (1%)
    all_gather x1, waiting for transfers between devices, shards(): columns_piece = lax.all_gather(right_environment, 'lb', axis=2, tiled=True)  116 us
    all_gather x1, waiting for transfers between devices, shards(): rows_piece = lax.all_gather(wavefunction, 'lb', axis=0, tiled=True)  101 us
    reduce_scatter x1, waiting for transfers between devices, shards(): lax.psum_scatter(partial_value.astype(jnp.bfloat16), 'rb', scatter_dimens...  60.5 us
    reshape x1, local copies, waits for them, and re-layouts, shards(): flat_piece = rows_piece.reshape(rows_piece.shape[0], 4 * local_right)  29.9 us
    dot_general x1, matrix products, shards(): jnp.dot(mixed_matrix, flat_piece, preferred_element_type=jnp.float32)  27.4 us
    dot_general x1, matrix products, shards(): jnp.dot(left_matrix, flat_piece, preferred_element_type=jnp.float32)  27.1 us
    ppermute x6, starting transfers between devices, shifted(): return lax.ppermute(value, axis, pairs)  24.4 us
    reduce_scatter x1, waiting for transfers between devices, shards(): lax.psum_scatter(full_rows.astype(jnp.bfloat16), 'rb', scatter_dimension=...  17.8 us
  transfers between devices with their start and end apart: 10, of which 5 were waited for; matrix products, arithmetic and copies ran while one was open for 18% of the time, Pallas kernels for 0%

commit v1 on v0

--- a/solution.py
+++ b/solution.py
@@ -6,6 +6,12 @@
 
 BOND_WIDTH = 3072
 SECTOR_TILES = 4
+
+
+def joined_along(parts, dim):
+    parts = jnp.moveaxis(parts, 0, dim)
+    dims = parts.shape
+    return parts.reshape(*dims[:dim], dims[dim] * dims[dim + 1], *dims[dim + 2 :])
 
 
 def shifted(value, axis, by):
@@ -43,7 +49,19 @@
     channels, row_count, full_bond = left_environment.shape
     local_right = wavefunction.shape[2]
     left_matrix = left_environment.reshape(channels * row_count, full_bond)
-    rows_piece = lax.all_gather(wavefunction, "lb", axis=0, tiled=True)
+    size = lax.axis_size("lb")
+    pairs_2 = [(i_2, (i_2 + 1) % size) for i_2 in range(size)]
+    back = [(b, a) for a, b in pairs_2]
+    lower, upper = ([], [])
+    for step in range(size - 1):
+        if step % 2 == 0:
+            lower.append(lax.ppermute(lower[-1] if lower else wavefunction, "lb", pairs_2))
+        else:
+            upper.append(lax.ppermute(upper[-1] if upper else wavefunction, "lb", back))
+    parts = jnp.stack([*lower[::-1], wavefunction, *upper])
+    shift = lax.axis_index("lb") - len(lower)
+    parts = parts[(jnp.arange(size) - shift) % size]
+    rows_piece = joined_along(parts, 0)
     flat_piece = rows_piece.reshape(rows_piece.shape[0], 4 * local_right)
     left_part = jnp.dot(left_matrix, flat_piece, preferred_element_type=jnp.float32)
     left_part = left_part.reshape(channels, row_count, 4, local_right)

time: 472 us -> 676 us (1.43); the launches traced: 471 us -> 668 us
  waiting for transfers between devices: 305 us -> 403 us
  local copies, waits for them, and re-layouts: 39.2 us -> 106 us
  starting transfers between devices: 24.6 us -> 39.6 us
  other arithmetic: 6.78 us -> 20.1 us
    ppermute x0 -> x7, waiting for transfers between devices: none -> 314 us  [the longest x4 314 us: shards(): lax.ppermute(lower[-1] if lower else wavefunction, 'lb', pairs_2)]
    all_gather x1, waiting for transfers between devices: 116 us -> 0.01 us  [shards(): columns_piece = lax.all_gather(right_environment, 'lb', axis=2, tiled=True)]
    all_gather x1 -> x0, waiting for transfers between devices: 101 us -> none  [shards(): rows_piece = lax.all_gather(wavefunction, 'lb', axis=0, tiled=True)]
    unnamed x13 -> x24, local copies, waits for them, and re-layouts: 4.68 us -> 48 us
    gather x0 -> x3, local copies, waits for them, and re-layouts: none -> 39.1 us  [shards(): parts = parts[(jnp.arange(size) - shift) % size]]
    reshape x1, local copies, waits for them, and re-layouts: 29.9 us -> 12.8 us  [shards(): left_part = left_part.reshape(channels, row_count, 4, local_right)]
    ppermute x0 -> x7, starting transfers between devices: none -> 13.6 us  [the longest x4 13.5 us: shards(): lax.ppermute(lower[-1] if lower else wavefunction, 'lb', pairs_2)]
    unnamed x0 -> x1, other arithmetic: none -> 13.3 us
  transfers between devices with their start and end apart: 10 -> 16, of which waited for: 5 -> 7; matrix products, arithmetic and copies ran while one was open for 18% -> 25% of each run, Pallas kernels for 0% -> 0%
where the time goes in v1:
time: 676 us; the launch traced here: 668 us
  waiting for transfers between devices  403 us (60%)
  local copies, waits for them, and re-layouts  106 us (16%)
  matrix products  73.3 us (11%)
  starting transfers between devices  39.6 us (6%)
  between operations  25.6 us (4%)
  other arithmetic  20.1 us (3%)
    ppermute x4, waiting for transfers between devices, shards(): lax.ppermute(lower[-1] if lower else wavefunction, 'lb', pairs_2)  314 us
    reduce_scatter x1, waiting for transfers between devices, shards(): lax.psum_scatter(partial_value.astype(jnp.bfloat16), 'rb', scatter_dimens...  63.4 us
    unnamed x24, local copies, waits for them, and re-layouts  48 us
    gather x3, local copies, waits for them, and re-layouts, shards(): parts = parts[(jnp.arange(size) - shift) % size]  39.1 us
    dot_general x1, matrix products, shards(): jnp.dot(left_matrix, flat_piece, preferred_element_type=jnp.float32)  28.2 us
    dot_general x1, matrix products, shards(): jnp.dot(mixed_matrix, flat_piece, preferred_element_type=jnp.float32)  27.7 us
    ppermute x6, starting transfers between devices, shifted(): return lax.ppermute(value, axis, pairs)  25.9 us
    reduce_scatter x1, waiting for transfers between devices, shards(): lax.psum_scatter(full_rows.astype(jnp.bfloat16), 'rb', scatter_dimension=...  16.6 us
  transfers between devices with their start and end apart: 16, of which 7 were waited for; matrix products, arithmetic and copies ran while one was open for 25% of the time, Pallas kernels for 0%

profile of v1, /device:TPU:0, one launch (start us, length us, event | category | flops | bytes accessed | tf_op | source)
XLA Modules:
  0.0 667.7 jit_solution(899621160277763903)
XLA Ops:
  7.2 0.7 all-gather.2.cloned.1.call-update
  8.5 46.7 %collective-permute-done = bf16[384,4,768]{2,1,0:T(4,128)(2,1)S(1)} collective-permute-done((bf16[384,4,768]{2,1,0:T(4,128)(2,1)}, bf16[384,4,768]{2,1,0:T(4,128)(2,1)S(1)}, u32[]{:S(2)}, u32[]{:S(2)}) %collective-permute-start) | collective-permute-done | bytes 2359328 | tf_op jit(solution)/shard_map/ppermute | solution.py:58
  55.2 1.4 copy-done.3
  56.6 3.0 collective-permute-start.1
  59.6 92.9 %collective-permute-done.1 = bf16[384,4,768]{2,1,0:T(4,128)(2,1)S(1)} collective-permute-done((bf16[384,4,768]{2,1,0:T(4,128)(2,1)S(1)}, bf16[384,4,768]{2,1,0:T(4,128)(2,1)S(1)}, u32[]{:S(2)}, u32[]{:S(2)}) %collective-permute-start.1) | collective-permute-done | bytes 2359328 | tf_op jit(solution)/shard_map/ppermute | solution.py:58
  152.5 1.5 copy-done.5
  154.0 4.9 collective-permute-start.2
  158.9 98.6 %collective-permute-done.2 = bf16[384,4,768]{2,1,0:T(4,128)(2,1)} collective-permute-done((bf16[384,4,768]{2,1,0:T(4,128)(2,1)S(1)}, bf16[384,4,768]{2,1,0:T(4,128)(2,1)}, u32[]{:S(2)}, u32[]{:S(2)}) %collective-permute-start.2) | collective-permute-done | bytes 2359328 | tf_op jit(solution)/shard_map/ppermute | solution.py:58
  257.5 5.0 collective-permute-start.3
  262.5 1.1 convolution_bitcast_fusion.1
  263.9 75.9 %collective-permute-done.3 = bf16[384,4,768]{2,1,0:T(4,128)(2,1)} collective-permute-done((bf16[384,4,768]{2,1,0:T(4,128)(2,1)}, bf16[384,4,768]{2,1,0:T(4,128)(2,1)}, u32[]{:S(2)}, u32[]{:S(2)}) %collective-permute-start.3) | collective-permute-done | bytes 2359328 | tf_op jit(solution)/shard_map/ppermute | solution.py:58
  339.7 2.5 bitcast_dynamic-update-slice_fusion.7
  342.2 2.7 bitcast_dynamic-update-slice_fusion.6
  344.9 2.7 bitcast_dynamic-update-slice_fusion.5
  347.6 1.0 bitcast_dynamic-update-slice_fusion.4
  348.7 1.0 bitcast_dynamic-update-slice_fusion.3
  349.7 2.7 bitcast_dynamic-update-slice_fusion.2
  352.4 2.7 bitcast_dynamic-update-slice_fusion.1
  355.1 1.0 bitcast_dynamic-update-slice_fusion
  356.2 11.4 %fusion.12 = (bf16[8,384,4,384]{3,2,1,0:T(4,128)(2,1)}, bf16[8,384,4,384]{3,2,1,0:T(4,128)(2,1)}) fusion(bf16[8,384,4,768]{3,2,1,0:T(4,128)(2,1)S(1)} %bitcast_dynamic-update-slice_fusion), kind=kLoop, calls=%fused_computation.58 | loop fusion | bytes 37748736 | tf_op jit(solution)/shard_map/gather | solution.py:63
  367.6 13.9 %gather_fusion.1 = bf16[8,384,4,384]{3,2,1,0:T(4,128)(2,1)} fusion(bf16[8,384,4,384]{3,2,1,0:T(4,128)(2,1)} %get-tuple-element.10, s32[1024]{0:T(1024)S(1)} %pad_clamp_fusion), kind=kCustom, calls=%fused_computation.1 | custom fusion | bytes 18874400 | tf_op jit(solution)/shard_map/gather | solution.py:63
  381.4 13.8 %gather_fusion = bf16[8,384,4,384]{3,2,1,0:T(4,128)(2,1)} fusion(bf16[8,384,4,384]{3,2,1,0:T(4,128)(2,1)} %get-tuple-element.9, s32[1024]{0:T(1024)S(1)} %pad_clamp_fusion), kind=kCustom, calls=%fused_computation | custom fusion | bytes 18874400 | tf_op jit(solution)/shard_map/gather | solution.py:63
  395.3 13.3 %pad_maximum_fusion = bf16[8,384,4,768]{3,2,1,0:T(4,128)(2,1)} fusion(bf16[8,384,4,384]{3,2,1,0:T(4,128)(2,1)} %gather_fusion.1, bf16[8,384,4,384]{3,2,1,0:T(4,128)(2,1)} %gather_fusion), kind=kLoop, calls=%fused_computation.2 | loop fusion | flops 37748736 | bytes 37748736
  408.6 12.9 %copy.34 = bf16[384,8,4,768]{3,1,2,0:T(8,128)(2,1)S(1)} copy(bf16[384,8,4,768]{3,2,1,0:T(4,128)(2,1)} %bitcast.67) | data formatting | bytes 37748736
  421.5 28.2 %convolution_bitcast_fusion = f32[384,8,8,128]{3,1,2,0:T(8,128)} fusion(bf16[3072,3072]{1,0:T(8,128)(2,1)S(1)} %bitcast.70, bf16[1024,3072]{1,0:T(8,128)(2,1)} %bitcast.75), kind=kOutput, calls=%fused_computation.5 | convolution fusion | flops 19327352832 | bytes 37748736 | tf_op jit(solution)/shard_map/dot_general | solution.py:66
  449.8 12.2 %copy.35 = f32[384,8,8,128]{3,2,1,0:T(8,128)} copy(f32[384,8,8,128]{3,1,2,0:T(8,128)} %convolution_bitcast_fusion) | data formatting | bytes 25165824
  461.9 12.8 %copy.24 = f32[8,128,4,768,1]{3,0,2,4,1:T(8,128)} copy(f32[8,128,4,768,1]{1,0,3,2,4:T(8,128)} %bitcast.68) | data formatting | bytes 25165824 | tf_op jit(solution)/shard_map/reshape | solution.py:67
  474.8 14.1 %bitcast_convert_fusion = bf16[128,768,8,4]{1,2,3,0:T(8,128)(2,1)S(1)} fusion(f32[8,128,4,768,1]{3,0,2,4,1:T(8,128)} %copy.24, f32[8,8,4,4,1]{1,0,3,2,4:T(8,128)S(1)} %bitcast.72), kind=kOutput, calls=%fused_computation.3 | convolution fusion | flops 1211105280 | bytes 18878464 | tf_op jit(solution)/shard_map/avyx,alxr->lyvr/dot_general | solution.py:69
  488.8 4.6 copy.36
  493.5 27.7 %convolution_convert_fusion = bf16[512,3072]{1,0:T(8,128)(2,1)} fusion(bf16[512,6144]{1,0:T(8,128)(2,1)} %bitcast.71, bf16[6144,3072]{1,0:T(8,128)(2,1)} %bitcast.74), kind=kOutput, calls=%fused_computation.4 | convolution fusion | flops 19328925696 | bytes 47185920 | tf_op jit(solution)/shard_map/dot_general | solution.py:75
  521.2 63.4 %reduce-scatter.3.cloned.1.call-done = bf16[512,768]{1,0:T(8,128)(2,1)} async-done(((bf16[512,3072]{1,0:T(8,128)(2,1)}), bf16[512,768]{1,0:T(8,128)(2,1)}) %reduce-scatter.3.cloned.1.call-update) | async-done | bytes 786448 | tf_op jit(solution)/shard_map/reduce_scatter | solution.py:76
  584.7 1.6 reshape_reshape.7
  586.2 1.3 collective-permute-start.7
  588.8 0.8 fusion.9
  591.5 1.3 collective-permute-start.9
  592.8 1.0 fusion
  594.3 9.9 %collective-permute-start.8 = (bf16[128,128]{1,0:T(8,128)(2,1)S(1)}, bf16[128,128]{1,0:T(8,128)(2,1)S(1)}, u32[]{:S(2)}, u32[]{:S(2)}) collective-permute-start(bf16[128,128]{1,0:T(8,128)(2,1)S(1)} %get-tuple-element.12), channel_id=1, source_target_pairs={{0,4},{4,8},{8,12},{12,16},{16,20},{20,24},{24,28},{1,5},{5,9},{9,... | collective-permute-start | bytes 98312 | tf_op jit(solution)/shard_map/ppermute | solution.py:20
  604.2 0.6 compare_reduce_fusion.4
  609.3 1.3 collective-permute-start.11
  610.8 8.2 %collective-permute-done.9 = bf16[128,3072]{1,0:T(8,128)(2,1)S(1)} collective-permute-done((bf16[128,3072]{1,0:T(8,128)(2,1)S(1)}, bf16[128,3072]{1,0:T(8,128)(2,1)S(1)}, u32[]{:S(2)}, u32[]{:S(2)}) %collective-permute-start.9) | collective-permute-done | bytes 786464 | tf_op jit(solution)/shard_map/ppermute | solution.py:20
  619.3 3.5 collective-permute-start.10
  622.8 0.6 compare_reduce_fusion.2
  628.3 8.7 %collective-permute-start.12 = (bf16[128,128]{1,0:T(8,128)(2,1)S(1)}, bf16[128,128]{1,0:T(8,128)(2,1)S(1)}, u32[]{:S(2)}, u32[]{:S(2)}) collective-permute-start(bf16[128,128]{1,0:T(8,128)(2,1)S(1)} %get-tuple-element.16), channel_id=1, source_target_pairs={{0,12},{4,16},{8,20},{12,24},{16,28},{1,13},{5,17},{9,21},{13,25},... | collective-permute-start | bytes 98312 | tf_op jit(solution)/shard_map/ppermute | solution.py:20
  637.0 0.6 compare_reduce_fusion
  639.7 0.7 slice.11
  640.5 2.4 reshape.76
  642.9 16.6 %reduce-scatter.5.cloned.1.call-done = bf16[128,256]{1,0:T(8,128)(2,1)} async-done(((bf16[128,1024]{1,0:T(8,128)(2,1)}), bf16[128,256]{1,0:T(8,128)(2,1)}) %reduce-scatter.5.cloned.1.call-update) | async-done | bytes 65552 | tf_op jit(solution)/shard_map/reduce_scatter | solution.py:102
  659.4 1.5 convert_multiply_fusion
  (50 shorter events, 5.1 us)
Async XLA Ops:
  7.2 255.4 %copy-start = (f32[8,8,2,2]{1,3,2,0:T(2,128)S(1)}, f32[8,8,2,2]{1,3,2,0:T(2,128)}, u32[]{:S(2)}) copy-start(f32[8,8,2,2]{1,3,2,0:T(2,128)} %param.8) | copy-start | bytes 3076
  7.2 341.5 %copy-start.2 = (bf16[384,4,768]{2,1,0:T(4,128)(2,1)S(1)}, bf16[384,4,768]{2,1,0:T(4,128)(2,1)}, u32[]{:S(2)}) copy-start(bf16[384,4,768]{2,1,0:T(4,128)(2,1)} %param.6) | copy-start | bytes 7077892
  7.2 486.3 %all-gather.2.cloned.1.call-start = ((), (), s32[]{:S(2)}) async-start(), calls=%async_computation.2 | async-start | bytes 42467328 | tf_op jit(solution)/shard_map/all_gather | solution.py:73
  7.9 576.7 %reduce-scatter.3.cloned.1.call-start = ((), (), s32[]{:S(2)}) async-start(), calls=%async_computation.3 | async-start | bytes 3932160 | tf_op jit(solution)/shard_map/reduce_scatter | solution.py:76
  8.0 47.2 %collective-permute-start = (bf16[384,4,768]{2,1,0:T(4,128)(2,1)}, bf16[384,4,768]{2,1,0:T(4,128)(2,1)S(1)}, u32[]{:S(2)}, u32[]{:S(2)}) collective-permute-start(bf16[384,4,768]{2,1,0:T(4,128)(2,1)} %param.6), channel_id=1, source_target_pairs={{0,4},{4,8},{8,12},{12,16},{16,20},{20,24},{24,28},{28,0},{1,5},{5... | collective-permute-start | bytes 7077896 | tf_op jit(solution)/shard_map/ppermute | solution.py:58
  55.2 1.4 copy-start.3
  56.6 95.9 %collective-permute-start.1 = (bf16[384,4,768]{2,1,0:T(4,128)(2,1)S(1)}, bf16[384,4,768]{2,1,0:T(4,128)(2,1)S(1)}, u32[]{:S(2)}, u32[]{:S(2)}) collective-permute-start(bf16[384,4,768]{2,1,0:T(4,128)(2,1)S(1)} %collective-permute-done), channel_id=1, source_target_pairs={{0,4},{4,8},{8,12},{12,16},{16,20},{20,24},{24,28},{28,0},{1,5},{5... | collective-permute-start | bytes 7077896 | tf_op jit(solution)/shard_map/ppermute | solution.py:58
  59.6 99.3 %collective-permute-start.4 = (bf16[384,4,768]{2,1,0:T(4,128)(2,1)}, bf16[384,4,768]{2,1,0:T(4,128)(2,1)}, u32[]{:S(2)}, u32[]{:S(2)}) collective-permute-start(bf16[384,4,768]{2,1,0:T(4,128)(2,1)} %param.6), channel_id=1, source_target_pairs={{4,0},{8,4},{12,8},{16,12},{20,16},{24,20},{28,24},{0,28},{5,1},{9... | collective-permute-start | bytes 7077896 | tf_op jit(solution)/shard_map/ppermute | solution.py:60
  152.5 1.5 copy-start.5
  154.0 103.5 %collective-permute-start.2 = (bf16[384,4,768]{2,1,0:T(4,128)(2,1)S(1)}, bf16[384,4,768]{2,1,0:T(4,128)(2,1)}, u32[]{:S(2)}, u32[]{:S(2)}) collective-permute-start(bf16[384,4,768]{2,1,0:T(4,128)(2,1)S(1)} %collective-permute-done.1), channel_id=1, source_target_pairs={{0,4},{4,8},{8,12},{12,16},{16,20},{20,24},{24,28},{28,0},{1,5},{5... | collective-permute-start | bytes 7077896 | tf_op jit(solution)/shard_map/ppermute | solution.py:58
  158.9 104.9 %collective-permute-start.5 = (bf16[384,4,768]{2,1,0:T(4,128)(2,1)}, bf16[384,4,768]{2,1,0:T(4,128)(2,1)}, u32[]{:S(2)}, u32[]{:S(2)}) collective-permute-start(bf16[384,4,768]{2,1,0:T(4,128)(2,1)} %collective-permute-done.4), channel_id=1, source_target_pairs={{4,0},{8,4},{12,8},{16,12},{20,16},{24,20},{28,24},{0,28},{5,1},{9... | collective-permute-start | bytes 7077896 | tf_op jit(solution)/shard_map/ppermute | solution.py:60
  257.5 82.2 %collective-permute-start.3 = (bf16[384,4,768]{2,1,0:T(4,128)(2,1)}, bf16[384,4,768]{2,1,0:T(4,128)(2,1)}, u32[]{:S(2)}, u32[]{:S(2)}) collective-permute-start(bf16[384,4,768]{2,1,0:T(4,128)(2,1)} %collective-permute-done.2), channel_id=1, source_target_pairs={{0,4},{4,8},{8,12},{12,16},{16,20},{20,24},{24,28},{28,0},{1,5},{5... | collective-permute-start | bytes 7077896 | tf_op jit(solution)/shard_map/ppermute | solution.py:58
  263.7 83.9 %copy-start.4 = (bf16[384,4,768]{2,1,0:T(4,128)(2,1)S(1)}, bf16[384,4,768]{2,1,0:T(4,128)(2,1)}, u32[]{:S(2)}) copy-start(bf16[384,4,768]{2,1,0:T(4,128)(2,1)} %copy-done.3) | copy-start | bytes 7077892
  263.8 91.3 %collective-permute-start.6 = (bf16[384,4,768]{2,1,0:T(4,128)(2,1)}, bf16[384,4,768]{2,1,0:T(4,128)(2,1)S(1)}, u32[]{:S(2)}, u32[]{:S(2)}) collective-permute-start(bf16[384,4,768]{2,1,0:T(4,128)(2,1)} %collective-permute-done.5), channel_id=1, source_target_pairs={{4,0},{8,4},{12,8},{16,12},{20,16},{24,20},{28,24},{0,28},{5,1},{9... | collective-permute-start | bytes 7077896 | tf_op jit(solution)/shard_map/ppermute | solution.py:60
  493.5 95.3 %copy-start.6 = (s32[8]{0:T(128)S(1)}, s32[8]{0:T(128)}, u32[]{:S(2)}) copy-start(s32[8]{0:T(128)} %param.11) | copy-start | bytes 100
  493.5 167.5 %copy-start.1 = (f32[8,8,2,2]{1,3,2,0:T(2,128)S(1)}, f32[8,8,2,2]{1,3,2,0:T(2,128)}, u32[]{:S(2)}) copy-start(f32[8,8,2,2]{1,3,2,0:T(2,128)} %param.8) | copy-start | bytes 3076
  521.2 138.3 %reduce-scatter.5.cloned.1.call-start = ((), (), s32[]{:S(2)}) async-start(), calls=%async_computation.4 | async-start | bytes 327680 | tf_op jit(solution)/shard_map/reduce_scatter | solution.py:102
  586.2 7.6 %collective-permute-start.7 = (bf16[128,3072]{1,0:T(8,128)(2,1)S(1)}, bf16[128,3072]{1,0:T(8,128)(2,1)S(1)}, u32[]{:S(2)}, u32[]{:S(2)}) collective-permute-start(bf16[128,3072]{1,0:T(8,128)(2,1)S(1)} %reshape_reshape.7), channel_id=1, source_target_pairs={{4,0},{8,4},{12,8},{16,12},{20,16},{24,20},{28,24},{5,1},{9,5},{13... | collective-permute-start | bytes 2359304 | tf_op jit(solution)/shard_map/ppermute | solution.py:20
  591.5 27.4 %collective-permute-start.9 = (bf16[128,3072]{1,0:T(8,128)(2,1)S(1)}, bf16[128,3072]{1,0:T(8,128)(2,1)S(1)}, u32[]{:S(2)}, u32[]{:S(2)}) collective-permute-start(bf16[128,3072]{1,0:T(8,128)(2,1)S(1)} %reshape_reshape.7), channel_id=1, source_target_pairs={{8,0},{12,4},{16,8},{20,12},{24,16},{28,20},{9,1},{13,5},{17,9},{2... | collective-permute-start | bytes 2359304 | tf_op jit(solution)/shard_map/ppermute | solution.py:20
  594.3 16.3 %collective-permute-start.8 = (bf16[128,128]{1,0:T(8,128)(2,1)S(1)}, bf16[128,128]{1,0:T(8,128)(2,1)S(1)}, u32[]{:S(2)}, u32[]{:S(2)}) collective-permute-start(bf16[128,128]{1,0:T(8,128)(2,1)S(1)} %get-tuple-element.12), channel_id=1, source_target_pairs={{0,4},{4,8},{8,12},{12,16},{16,20},{20,24},{24,28},{1,5},{5,9},{9,... | collective-permute-start | bytes 98312 | tf_op jit(solution)/shard_map/ppermute | solution.py:20
  609.3 18.6 %collective-permute-start.11 = (bf16[128,3072]{1,0:T(8,128)(2,1)S(1)}, bf16[128,3072]{1,0:T(8,128)(2,1)S(1)}, u32[]{:S(2)}, u32[]{:S(2)}) collective-permute-start(bf16[128,3072]{1,0:T(8,128)(2,1)S(1)} %reshape_reshape.7), channel_id=1, source_target_pairs={{12,0},{16,4},{20,8},{24,12},{28,16},{13,1},{17,5},{21,9},{25,13},... | collective-permute-start | bytes 2359304 | tf_op jit(solution)/shard_map/ppermute | solution.py:20
  619.3 8.4 %collective-permute-start.10 = (bf16[128,128]{1,0:T(8,128)(2,1)S(1)}, bf16[128,128]{1,0:T(8,128)(2,1)S(1)}, u32[]{:S(2)}, u32[]{:S(2)}) collective-permute-start(bf16[128,128]{1,0:T(8,128)(2,1)S(1)} %get-tuple-element.14), channel_id=1, source_target_pairs={{0,8},{4,12},{8,16},{12,20},{16,24},{20,28},{1,9},{5,13},{9,17},{1... | collective-permute-start | bytes 98312 | tf_op jit(solution)/shard_map/ppermute | solution.py:20
  628.3 11.2 %collective-permute-start.12 = (bf16[128,128]{1,0:T(8,128)(2,1)S(1)}, bf16[128,128]{1,0:T(8,128)(2,1)S(1)}, u32[]{:S(2)}, u32[]{:S(2)}) collective-permute-start(bf16[128,128]{1,0:T(8,128)(2,1)S(1)} %get-tuple-element.16), channel_id=1, source_target_pairs={{0,12},{4,16},{8,20},{12,24},{16,28},{1,13},{5,17},{9,21},{13,25},... | collective-permute-start | bytes 98312 | tf_op jit(solution)/shard_map/ppermute | solution.py:20
Sparse Core Ops, SparseCore 0:
  9.9 309.2 all-gather.1
  521.3 63.3 reduce-scatter.2
  640.6 18.7 reduce-scatter.4
